TPU v7x, 512 devices: a whole 4x8x8 slice. The times are simulated.
512 devices in a mesh: ctx: 64 (over y_hi, z, core), ch: 8 (over y_lo, x).
Axes of the slice: x: 4, y: 8 (y_hi: 4, y_lo: 2; y = y_hi * 2 + y_lo), z: 8, core: 2. Of those that a mesh axis runs over, the one named last changes fastest.
Arguments:
- query_proj: bfloat16 [8192, 4096], P('ctx', 'ch'), may hold values from -6 to 6
- key_proj: bfloat16 [8192, 4096], P('ctx', 'ch'), may hold values from -6 to 6
- value_proj: bfloat16 [8192, 4096], P('ctx', 'ch'), may hold values from -6 to 6
- output_grad: bfloat16 [8192, 4096], P('ctx', 'ch'), may hold values from -6 to 6
- residue: float32 [4096, 16], P(('ch', 'ctx')), may hold values from -5 to 5
- decay_rate: float32 [4096, 16], P(('ch', 'ctx')), may hold values from 1.2207031e-05 to 0.0625
Outputs:
- query_grad: bfloat16 [8192, 4096], P('ctx', 'ch')
- key_grad: bfloat16 [8192, 4096], P('ctx', 'ch')
- value_grad: bfloat16 [8192, 4096], P('ctx', 'ch')
- residue_grad: float32 [4096, 16], P(('ch', 'ctx'))
- log_rate_grad: float32 [4096, 16], P(('ch', 'ctx'))
All inputs are finite; a program needn't handle non-finite values.
Results may differ from a plain program's by a relative error of at most 0.0085.
Values may be sent and summed in bfloat16 or wider, within the bound.
A program may use at most 64 MiB of HBM per device.

v0:
```python
import functools
import math

import jax
import jax.numpy as jnp
from jax import lax
from jax.experimental import pallas as pl
from jax.experimental.pallas import tpu as pltpu
from jax.sharding import PartitionSpec as P

MESH = pl.DeviceIdType.MESH
F32 = jnp.float32
BF16 = jnp.bfloat16
HIGHEST = lax.Precision.HIGHEST
BLOCK = 128
OWN = 8
LANES = 128


def dot(left, right, dims=((1,), (0,)), precision=None):
    return lax.dot_general(
        left, right, (dims, ((), ())), precision=precision, preferred_element_type=F32
    )


def split(value):
    high = value.astype(BF16)
    return high, (value - high.astype(F32)).astype(BF16)


def iota(shape, axis):
    return lax.broadcasted_iota(jnp.int32, shape, axis)


def shift_rows(value, step, down):
    rows = value.shape[0]
    index = iota(value.shape, 0)
    if down:
        return jnp.where(index >= step, pltpu.roll(value, step, 0), 0.0)
    return jnp.where(index < rows - step, pltpu.roll(value, rows - step, 0), 0.0)


def scan_blocks(state, rate_row, down):
    step = 1
    while step < state.shape[0]:
        decay = jnp.exp(rate_row * (-float(BLOCK * step)))
        state = state + decay * shift_rows(state, step, down)
        step *= 2
    return shift_rows(state, 1, down)


def scan_moments(state, moment, rate_row):
    step = 1
    while step < state.shape[0]:
        decay = jnp.exp(rate_row * (-float(BLOCK * step)))
        below = shift_rows(state, step, True)
        moment = moment + decay * (
            shift_rows(moment, step, True) + float(BLOCK * step) * below
        )
        state = state + decay * below
        step *= 2
    return shift_rows(state, 1, True), shift_rows(moment, 1, True)


def own_rows(stacked, blocks):
    group = iota((blocks, LANES), 1) // 16
    total = jnp.zeros((blocks, LANES), F32)
    for channel in range(OWN):
        part = stacked[channel * blocks : (channel + 1) * blocks]
        total = jnp.where(group == channel, part, total)
    return total


def kernel(
    sizes,
    scale,
    query_ref,
    key_ref,
    value_ref,
    upstream_ref,
    residue_ref,
    rate_ref,
    out_ref,
    grad_ref,
    residue_grad_ref,
    rate_grad_ref,
    query_in,
    key_in,
    value_in,
    upstream_in,
    send_a,
    recv_a,
    send_b,
    recv_b,
    wide,
    xs,
    gs,
    toep_hi,
    toep_lo,
    tables,
    in_sems,
    send_sems,
    recv_sems,
):
    blocks_y, blocks_z = sizes
    blocks = blocks_y * blocks_z * 2
    me = lax.axis_index("ctx")
    my_core = lax.rem(me, 2)
    my_z = lax.rem(me // 2, blocks_z)
    my_y = me // (2 * blocks_z)

    def peer_of(step):
        step_z = lax.rem(step, blocks_z)
        rest = step // blocks_z
        step_core = lax.rem(rest, 2)
        step_y = rest // 2
        half_z = (step_z + 1) // 2
        delta_z = blocks_z // 2 + (1 - 2 * lax.rem(step_z, 2)) * half_z + blocks_z
        delta_y = blocks_y - 1 - step_y
        z = lax.rem(my_z + delta_z, blocks_z)
        y = lax.rem(my_y + delta_y, blocks_y)
        core = lax.rem(my_core + 1 + step_core, 2)
        return (y * blocks_z + z) * 2 + core

    barrier = pltpu.get_barrier_semaphore()

    def greet(step, carry):
        pl.semaphore_signal(
            barrier, inc=1, device_id={"ctx": peer_of(step)}, device_id_type=MESH
        )
        return carry

    lax.fori_loop(0, blocks - 1, greet, 0)

    loads = []
    for place, (source, target) in enumerate(
        ((key_ref, key_in), (value_ref, value_in), (query_ref, query_in), (upstream_ref, upstream_in))
    ):
        load = pltpu.make_async_copy(source, target, in_sems.at[place])
        load.start()
        loads.append(load)

    rate = rate_ref[...]
    residue = residue_ref[...]
    spread = (iota((16, LANES), 1) % 16 == iota((16, LANES), 0)).astype(F32)
    own_lane = iota((OWN, LANES), 1) // 16 == iota((OWN, LANES), 0)

    def to_row(params):
        tiled = dot(params, spread, precision=HIGHEST)
        return jnp.sum(jnp.where(own_lane, tiled, 0.0), axis=0, keepdims=True)

    rate_row = to_row(rate)
    gain_row = to_row(residue * jnp.sqrt(rate))

    for load in loads:
        load.wait()
    channels = blocks * OWN
    for first in range(0, channels, LANES):
        cols = pl.ds(first, LANES)
        gated = (key_in[:, cols].astype(F32) * value_in[:, cols].astype(F32)).astype(BF16)
        gate_grad = (upstream_in[:, cols].astype(F32) * query_in[:, cols].astype(F32)).astype(BF16)
        gated = jnp.transpose(gated.astype(F32)).reshape(LANES // OWN, OWN, BLOCK)
        gate_grad = jnp.transpose(gate_grad.astype(F32)).reshape(LANES // OWN, OWN, BLOCK)
        send_a[pl.ds(first // OWN, LANES // OWN)] = jnp.concatenate(
            [gated, gate_grad], axis=1
        ).astype(BF16)

    pl.semaphore_wait(barrier, blocks - 1)

    def exchange(send, recv, phase):
        def push(step, carry):
            peer = peer_of(step)
            pltpu.make_async_remote_copy(
                src_ref=send.at[peer],
                dst_ref=recv.at[me],
                send_sem=send_sems.at[phase],
                recv_sem=recv_sems.at[phase],
                device_id={"ctx": peer},
                device_id_type=MESH,
            ).start()
            return carry

        lax.fori_loop(0, blocks - 1, push, 0)
        pltpu.make_async_copy(send.at[me], recv.at[me], recv_sems.at[phase]).start()

    def arrived(recv, phase):
        pltpu.make_async_copy(recv, recv, recv_sems.at[phase]).wait()

    def sent(send, phase):
        rest = send.at[pl.ds(0, blocks - 1)]
        pltpu.make_async_copy(rest, rest, send_sems.at[phase]).wait()

    exchange(send_a, recv_a, 0)

    place_row = iota((BLOCK, LANES), 0).astype(F32)
    place_lane = iota((OWN, LANES), 1).astype(F32)
    ahead = jnp.exp(-rate_row * (float(BLOCK - 1) - place_row))
    behind = jnp.exp(-rate_row * (place_row + 1.0))
    for place, table in enumerate((ahead, behind, gain_row * behind, gain_row * ahead)):
        high, low = split(table)
        tables[2 * place] = high
        tables[2 * place + 1] = low
    taps = jnp.zeros((OWN, LANES), F32)
    for mode in range(16):
        mode_rate = rate[:, mode : mode + 1]
        taps = taps + residue[:, mode : mode + 1] * (
            jnp.sqrt(mode_rate) * jnp.exp(-mode_rate * place_lane)
        )
    causal = iota((BLOCK, BLOCK), 1) >= iota((BLOCK, BLOCK), 0)
    for channel in range(OWN):
        row = jnp.broadcast_to(taps[channel : channel + 1], (BLOCK, LANES))
        row = pltpu.roll(row, 0, 1, stride=1, stride_axis=0)
        high, low = split(jnp.where(causal, row, 0.0))
        toep_hi[channel] = high
        toep_lo[channel] = low

    arrived(recv_a, 0)
    wide[...] = recv_a[...].astype(F32).reshape(blocks * 16, BLOCK)
    for channel in range(OWN):
        rows = pl.ds(channel * blocks, blocks)
        xs[rows, :] = wide[pl.ds(channel, blocks, stride=16), :].astype(BF16)
        gs[rows, :] = wide[pl.ds(OWN + channel, blocks, stride=16), :].astype(BF16)
    x_all = xs[...]
    g_all = gs[...]
    x_ends = own_rows(dot(x_all, tables[0]) + dot(x_all, tables[1]), blocks)
    g_ends = own_rows(dot(g_all, tables[2]) + dot(g_all, tables[3]), blocks)
    x_state = scan_blocks(x_ends, rate_row, True)
    g_state = scan_blocks(g_ends, rate_row, False)
    group = iota((blocks, LANES), 1) // 16

    def carried(state, high, low):
        parts = jnp.concatenate(
            [jnp.where(group == channel, state, 0.0) for channel in range(OWN)], axis=0
        )
        part_hi, part_lo = split(parts)
        over = ((1,), (1,))
        return dot(part_hi, high, over) + dot(part_lo, high, over) + dot(part_hi, low, over)

    x_carried = carried(x_state, tables[4], tables[5])
    g_carried = carried(g_state, tables[6], tables[7])
    for channel in range(OWN):
        rows = slice(channel * blocks, (channel + 1) * blocks)
        x_own = x_all[rows]
        g_own = g_all[rows]
        high = toep_hi[channel]
        low = toep_lo[channel]
        over = ((1,), (1,))
        wide[pl.ds(channel, blocks, stride=16), :] = (
            dot(x_own, high) + dot(x_own, low) + x_carried[rows]
        )
        wide[pl.ds(OWN + channel, blocks, stride=16), :] = (
            dot(g_own, high, over) + dot(g_own, low, over) + g_carried[rows]
        )
    send_b[...] = wide[...].reshape(blocks, 16, BLOCK).astype(BF16)
    exchange(send_b, recv_b, 1)

    high, low = split(ahead * (float(BLOCK - 1) - place_row))
    x_slopes = own_rows(dot(x_all, high) + dot(x_all, low), blocks)
    high, low = split(behind * (place_row + 1.0))
    g_slopes = own_rows(dot(g_all, high) + dot(g_all, low), blocks)
    x_state, x_moment = scan_moments(x_ends, x_slopes, rate_row)
    plain = jnp.sum(g_ends * x_state, axis=0, keepdims=True)
    sloped = jnp.sum(g_ends * x_moment + g_slopes * x_state, axis=0, keepdims=True)
    reverse = (iota((BLOCK, BLOCK), 0) + iota((BLOCK, BLOCK), 1) == BLOCK - 1).astype(BF16)
    x_reversed = dot(x_all, reverse).astype(BF16)
    paired = iota((BLOCK, BLOCK), 0) + iota((BLOCK, BLOCK), 1) >= BLOCK - 1
    lags = []
    for channel in range(OWN):
        rows = slice(channel * blocks, (channel + 1) * blocks)
        pairs = dot(g_all[rows], x_reversed[rows], ((0,), (0,)))
        pairs = jnp.where(paired, pairs, 0.0)
        pairs = pltpu.roll(pairs, 1, 1, stride=1, stride_axis=0)
        lags.append(jnp.sum(pairs, axis=0, keepdims=True))
    lags = jnp.concatenate(lags, axis=0)
    decays = jnp.exp(-rate_row * place_row)

    def own_sum(table):
        full = dot(lags, table, precision=HIGHEST)
        return jnp.sum(jnp.where(own_lane, full, 0.0), axis=0, keepdims=True)

    plain = plain + own_sum(decays)
    sloped = sloped + own_sum(decays * place_row)
    root_row = jnp.sqrt(rate_row) * scale
    residue_row = to_row(residue)
    gather = (iota((LANES, 16), 0) % 16 == iota((LANES, 16), 1)).astype(F32)

    def from_row(row):
        rows = jnp.where(own_lane, jnp.broadcast_to(row, (OWN, LANES)), 0.0)
        return dot(rows, gather, precision=HIGHEST)

    residue_grad_ref[...] = from_row(root_row * plain)
    rate_grad_ref[...] = from_row(root_row * residue_row * (0.5 * plain - rate_row * sloped))

    arrived(recv_b, 1)
    for first in range(0, channels, LANES):
        cols = pl.ds(first, LANES)
        both = recv_b[pl.ds(first // OWN, LANES // OWN)].astype(F32)
        out_ref[:, cols] = jnp.transpose(both[:, :OWN].reshape(LANES, BLOCK)).astype(BF16)
        grad_ref[:, cols] = jnp.transpose(both[:, OWN:].reshape(LANES, BLOCK)).astype(BF16)
    sent(send_a, 0)
    sent(send_b, 1)


def times_bf16(left, right):
    return (left.astype(F32) * right.astype(F32)).astype(BF16)


def local(sizes, query_proj, key_proj, value_proj, output_grad, residue, decay_rate):
    tok_dev, channels = query_proj.shape
    blocks = sizes[0] * sizes[1] * 2
    scale = float(tok_dev * blocks) ** (-0.5)
    anywhere = pl.BlockSpec(memory_space=pl.ANY)
    vmem = pl.BlockSpec(memory_space=pltpu.VMEM)
    tokens = jax.ShapeDtypeStruct((tok_dev, channels), BF16)
    params = jax.ShapeDtypeStruct(residue.shape, F32)
    message = pltpu.VMEM((blocks, 16, BLOCK), BF16)
    conv_out, conv_grad, residue_grad, rate_grad = pl.pallas_call(
        functools.partial(kernel, sizes, scale),
        out_shape=(tokens, tokens, params, params),
        in_specs=[anywhere] * 4 + [vmem] * 2,
        out_specs=[vmem] * 4,
        scratch_shapes=[pltpu.VMEM((tok_dev, channels), BF16)] * 4
        + [message] * 4
        + [
            pltpu.VMEM((blocks * 16, BLOCK), F32),
            pltpu.VMEM((blocks * OWN, BLOCK), BF16),
            pltpu.VMEM((blocks * OWN, BLOCK), BF16),
            pltpu.VMEM((OWN, BLOCK, BLOCK), BF16),
            pltpu.VMEM((OWN, BLOCK, BLOCK), BF16),
            pltpu.VMEM((8, BLOCK, LANES), BF16),
            pltpu.SemaphoreType.DMA((4,)),
            pltpu.SemaphoreType.DMA((2,)),
            pltpu.SemaphoreType.DMA((2,)),
        ],
        compiler_params=pltpu.CompilerParams(collective_id=0, has_side_effects=True),
    )(query_proj, key_proj, value_proj, output_grad, residue, decay_rate)
    query_grad = times_bf16(output_grad, conv_out)
    key_grad = times_bf16(conv_grad, value_proj)
    value_grad = times_bf16(conv_grad, key_proj)
    return query_grad, key_grad, value_grad, residue_grad, rate_grad


def solution(mesh):
    ranks = mesh.shape["ctx"]
    along_z = min(8, ranks // 2)
    sizes = (ranks // (2 * along_z), along_z)
    tokens = P("ctx", "ch")
    params = P(("ch", "ctx"), None)
    return jax.shard_map(
        functools.partial(local, sizes),
        mesh=mesh,
        in_specs=(tokens,) * 4 + (params,) * 2,
        out_specs=(tokens,) * 3 + (params,) * 2,
        check_vma=False,
    )
```

profile of v0, /device:TPU:1, one launch (start us, length us, event | category | flops | bytes accessed | tf_op | source)
XLA Modules:
  0.0 43.7 jit_solution(890197362870419759)
XLA Ops:
  0.6 0.0 copy-start.2
  0.6 0.0 copy-start.1
  0.7 0.0 copy-start
  0.7 39.3 %shard_map.101 = (bf16[128,512]{1,0:T(8,128)(2,1)}, bf16[128,512]{1,0:T(8,128)(2,1)}, f32[8,16]{1,0:T(8,128)}, f32[8,16]{1,0:T(8,128)}) custom-call(bf16[128,512]{1,0:T(8,128)(2,1)} %query_ref.1, bf16[128,512]{1,0:T(8,128)(2,1)} %key_ref.1, bf16[128,512]{1,0:T(8,128)(2,1)} %value_ref.1, bf16[128,512]{1,0:T(8,128)(2,1)} %upstream_ref.1, f32[8,16]{1,0:T(8,128)} %residue_ref.1, ...), custom_call_target="tpu_custom_call" | custom-call | tf_op jit(solution)/shard_map/pallas_call | solution.py:317
  39.9 0.0 copy-done.2
  39.9 0.0 copy-done.1
  40.0 0.0 copy-done
  40.0 1.8 %fusion.1 = (bf16[128,512]{1,0:T(8,128)(2,1)}, bf16[128,512]{1,0:T(8,128)(2,1)}, bf16[128,512]{1,0:T(8,128)(2,1)}) fusion(bf16[128,512]{1,0:T(8,128)(2,1)} %get-tuple-element.10, bf16[128,512]{1,0:T(8,128)(2,1)S(1)} %copy-done, bf16[128,512]{1,0:T(8,128)(2,1)S(1)} %copy-done.1, bf16[128,512]{1,0:T(8,128)(2,1)} %get-tuple-element.9, ...), kind=kLoop, calls=%fused_computation.3 | loop fusion | flops 720896 | bytes 1048576 | tf_op jit(solution)/shard_map/convert_element_type | solution.py:305
  41.7 0.0 copy-start.4
  41.7 0.7 %copy-done.4 = f32[8,16]{1,0:T(8,128)S(1)} copy-done((f32[8,16]{1,0:T(8,128)S(1)}, f32[8,16]{1,0:T(8,128)}, u32[]{:S(2)}) %copy-start.4) | copy-done | bytes 536
  42.4 0.0 copy-start.3
  42.4 0.6 %copy.13 = f32[8,16]{1,0:T(8,128)} copy(f32[8,16]{1,0:T(8,128)S(1)} %copy-done.4) | data formatting | bytes 1024
  43.0 0.1 copy-done.3
  43.1 0.6 %copy.14 = f32[8,16]{1,0:T(8,128)} copy(f32[8,16]{1,0:T(8,128)S(1)} %copy-done.3) | data formatting | bytes 1024
Async XLA Ops:
  0.6 39.3 %copy-start.2 = (bf16[128,512]{1,0:T(8,128)(2,1)S(1)}, bf16[128,512]{1,0:T(8,128)(2,1)}, u32[]{:S(2)}) copy-start(bf16[128,512]{1,0:T(8,128)(2,1)} %upstream_ref.1) | copy-start | bytes 393220
  0.6 39.3 %copy-start.1 = (bf16[128,512]{1,0:T(8,128)(2,1)S(1)}, bf16[128,512]{1,0:T(8,128)(2,1)}, u32[]{:S(2)}) copy-start(bf16[128,512]{1,0:T(8,128)(2,1)} %value_ref.1) | copy-start | bytes 393220
  0.7 39.3 %copy-start = (bf16[128,512]{1,0:T(8,128)(2,1)S(1)}, bf16[128,512]{1,0:T(8,128)(2,1)}, u32[]{:S(2)}) copy-start(bf16[128,512]{1,0:T(8,128)(2,1)} %key_ref.1) | copy-start | bytes 393220
  41.7 0.7 %copy-start.4 = (f32[8,16]{1,0:T(8,128)S(1)}, f32[8,16]{1,0:T(8,128)}, u32[]{:S(2)}) copy-start(f32[8,16]{1,0:T(8,128)} %get-tuple-element.24) | copy-start | bytes 1540
  42.4 0.7 %copy-start.3 = (f32[8,16]{1,0:T(8,128)S(1)}, f32[8,16]{1,0:T(8,128)}, u32[]{:S(2)}) copy-start(f32[8,16]{1,0:T(8,128)} %get-tuple-element.25) | copy-start | bytes 1540
where the time goes:
time: 44.5 us; the launch traced here: 43.7 us
  Pallas kernels  39.3 us (88%)
  local copies, waits for them, and re-layouts  1.96 us (4%)
  other arithmetic  1.77 us (4%)
  between operations  0.69 us (2%)
    pallas_call x1, Pallas kernels, local(): pl.pallas_call(functools.partial(kernel, sizes, scale), out_shape=(tokens...  39.3 us
    unnamed x12, local copies, waits for them, and re-layouts  1.96 us
    convert_element_type x1, other arithmetic, times_bf16(): return (left.astype(F32) * right.astype(F32)).astype(BF16)  1.77 us

commit v1 on v0

--- a/solution.py
+++ b/solution.py
@@ -301,8 +301,48 @@
     sent(send_b, 1)
 
 
-def times_bf16(left, right):
-    return (left.astype(F32) * right.astype(F32)).astype(BF16)
+def finish(
+    upstream_ref,
+    value_ref,
+    key_ref,
+    out_ref,
+    grad_ref,
+    residue_grad_ref,
+    rate_grad_ref,
+    query_grad_hbm,
+    key_grad_hbm,
+    value_grad_hbm,
+    residue_grad_hbm,
+    rate_grad_hbm,
+    query_grad,
+    key_grad,
+    value_grad,
+    out_sems,
+):
+    stores = [
+        pltpu.make_async_copy(source, target, out_sems.at[place])
+        for place, (source, target) in enumerate(
+            (
+                (query_grad, query_grad_hbm),
+                (key_grad, key_grad_hbm),
+                (value_grad, value_grad_hbm),
+                (residue_grad_ref, residue_grad_hbm),
+                (rate_grad_ref, rate_grad_hbm),
+            )
+        )
+    ]
+    stores[3].start()
+    stores[4].start()
+    products = (
+        (upstream_ref, out_ref, query_grad),
+        (value_ref, grad_ref, key_grad),
+        (key_ref, grad_ref, value_grad),
+    )
+    for store, (gate, result, target) in zip(stores, products):
+        target[...] = (gate[...].astype(F32) * result[...].astype(F32)).astype(BF16)
+        store.start()
+    for store in stores:
+        store.wait()
 
 
 def local(sizes, query_proj, key_proj, value_proj, output_grad, residue, decay_rate):
@@ -314,9 +354,11 @@
     tokens = jax.ShapeDtypeStruct((tok_dev, channels), BF16)
     params = jax.ShapeDtypeStruct(residue.shape, F32)
     message = pltpu.VMEM((blocks, 16, BLOCK), BF16)
+    tokens_vmem = pltpu.VMEM(tokens.shape, BF16)
+    params_vmem = pltpu.VMEM(params.shape, F32)
     conv_out, conv_grad, residue_grad, rate_grad = pl.pallas_call(
         functools.partial(kernel, sizes, scale),
-        out_shape=(tokens, tokens, params, params),
+        out_shape=(tokens_vmem, tokens_vmem, params_vmem, params_vmem),
         in_specs=[anywhere] * 4 + [vmem] * 2,
         out_specs=[vmem] * 4,
         scratch_shapes=[pltpu.VMEM((tok_dev, channels), BF16)] * 4
@@ -332,12 +374,17 @@
             pltpu.SemaphoreType.DMA((2,)),
             pltpu.SemaphoreType.DMA((2,)),
         ],
-        compiler_params=pltpu.CompilerParams(collective_id=0, has_side_effects=True),
+        compiler_params=pltpu.CompilerParams(collective_id=0, has_side_effects=True, vmem_limit_bytes=60 * 1024 * 1024),
     )(query_proj, key_proj, value_proj, output_grad, residue, decay_rate)
-    query_grad = times_bf16(output_grad, conv_out)
-    key_grad = times_bf16(conv_grad, value_proj)
-    value_grad = times_bf16(conv_grad, key_proj)
-    return query_grad, key_grad, value_grad, residue_grad, rate_grad
+    return pl.pallas_call(
+        finish,
+        out_shape=(tokens,) * 3 + (params,) * 2,
+        in_specs=[vmem] * 7,
+        out_specs=[anywhere] * 5,
+        scratch_shapes=[pltpu.VMEM((tok_dev, channels), BF16)] * 3
+        + [pltpu.SemaphoreType.DMA((5,))],
+        compiler_params=pltpu.CompilerParams(vmem_limit_bytes=8 << 20),
+    )(output_grad, value_proj, key_proj, conv_out, conv_grad, residue_grad, rate_grad)
 
 
 def solution(mesh):

time: 44.5 us -> 40.8 us (0.917)
  local copies, waits for them, and re-layouts: 1.96 us -> 0.01 us
  other arithmetic: 1.77 us -> 0 us
    unnamed x12 -> x6, local copies, waits for them, and re-layouts: 1.96 us -> 0.01 us
    convert_element_type x1 -> x0, other arithmetic: 1.77 us -> none  [times_bf16(): return (left.astype(F32) * right.astype(F32)).astype(BF16)]
    pallas_call x0 -> x1, Pallas kernels: none -> 0.82 us  [local(): pl.pallas_call(finish, out_shape=(tokens,) * 3 + (params,) * 2, in_specs=...]
    pallas_call x1, Pallas kernels: 39.3 us -> 38.6 us  [local(): pl.pallas_call(functools.partial(kernel, sizes, scale), out_shape=(tokens...]
where the time goes in v1:
time: 40.8 us; the launch traced here: 40.1 us
  Pallas kernels  39.4 us (97%)
  between operations  0.69 us (2%)
    pallas_call x1, Pallas kernels, local(): pl.pallas_call(functools.partial(kernel, sizes, scale), out_shape=(tokens...  38.6 us
    pallas_call x1, Pallas kernels, local(): pl.pallas_call(finish, out_shape=(tokens,) * 3 + (params,) * 2, in_specs=...  0.82 us

profile of v1, /device:TPU:1, one launch (start us, length us, event | category | flops | bytes accessed | tf_op | source)
XLA Modules:
  0.0 40.1 jit_solution(11316323317498864929)
XLA Ops:
  0.6 0.0 copy-start
  0.6 0.0 copy-start.1
  0.7 0.0 copy-start.2
  0.7 38.6 %shard_map.101 = (bf16[128,512]{1,0:T(8,128)(2,1)S(1)}, bf16[128,512]{1,0:T(8,128)(2,1)S(1)}, f32[8,16]{1,0:T(8,128)S(1)}, f32[8,16]{1,0:T(8,128)S(1)}) custom-call(bf16[128,512]{1,0:T(8,128)(2,1)} %query_ref.1, bf16[128,512]{1,0:T(8,128)(2,1)} %key_ref.3, bf16[128,512]{1,0:T(8,128)(2,1)} %value_ref.3, bf16[128,512]{1,0:T(8,128)(2,1)} %upstream_ref.3, ...), custom_call_target="tpu_custom_call" | custom-call | tf_op jit(solution)/shard_map/pallas_call | solution.py:359
  39.2 0.0 copy-done
  39.2 0.0 copy-done.1
  39.3 0.0 copy-done.2
  39.3 0.8 %shard_map.102 = (bf16[128,512]{1,0:T(8,128)(2,1)}, bf16[128,512]{1,0:T(8,128)(2,1)}, bf16[128,512]{1,0:T(8,128)(2,1)}, f32[8,16]{1,0:T(8,128)}, f32[8,16]{1,0:T(8,128)}) custom-call(bf16[128,512]{1,0:T(8,128)(2,1)S(1)} %copy-done, bf16[128,512]{1,0:T(8,128)(2,1)S(1)} %copy-done.1, bf16[128,512]{1,0:T(8,128)(2,1)S(1)} %copy-done.2, ...), custom_call_target="tpu_custom_call" | custom-call | tf_op jit(solution)/shard_map/pallas_call | solution.py:379
Async XLA Ops:
  0.6 38.6 %copy-start = (bf16[128,512]{1,0:T(8,128)(2,1)S(1)}, bf16[128,512]{1,0:T(8,128)(2,1)}, u32[]{:S(2)}) copy-start(bf16[128,512]{1,0:T(8,128)(2,1)} %upstream_ref.3) | copy-start | bytes 393220
  0.6 38.6 %copy-start.1 = (bf16[128,512]{1,0:T(8,128)(2,1)S(1)}, bf16[128,512]{1,0:T(8,128)(2,1)}, u32[]{:S(2)}) copy-start(bf16[128,512]{1,0:T(8,128)(2,1)} %value_ref.3) | copy-start | bytes 393220
  0.7 38.6 %copy-start.2 = (bf16[128,512]{1,0:T(8,128)(2,1)S(1)}, bf16[128,512]{1,0:T(8,128)(2,1)}, u32[]{:S(2)}) copy-start(bf16[128,512]{1,0:T(8,128)(2,1)} %key_ref.3) | copy-start | bytes 393220

commit v2 on v1

--- a/solution.py
+++ b/solution.py
@@ -101,6 +101,8 @@
     in_sems,
     send_sems,
     recv_sems,
+    ready_sem,
+    relay_sem,
 ):
     blocks_y, blocks_z = sizes
     blocks = blocks_y * blocks_z * 2
@@ -109,28 +111,35 @@
     my_z = lax.rem(me // 2, blocks_z)
     my_y = me // (2 * blocks_z)
 
-    def peer_of(step):
-        step_z = lax.rem(step, blocks_z)
-        rest = step // blocks_z
-        step_core = lax.rem(rest, 2)
-        step_y = rest // 2
-        half_z = (step_z + 1) // 2
-        delta_z = blocks_z // 2 + (1 - 2 * lax.rem(step_z, 2)) * half_z + blocks_z
-        delta_y = blocks_y - 1 - step_y
-        z = lax.rem(my_z + delta_z, blocks_z)
-        y = lax.rem(my_y + delta_y, blocks_y)
-        core = lax.rem(my_core + 1 + step_core, 2)
+    half = blocks_z // 2
+    members = blocks // 2
+    my_base = (my_z // half) * half
+    is_first = my_z < half
+
+    def peer_of(base, step):
+        delta_z = lax.rem(step, half)
+        rest = step // half
+        z = base + lax.rem(lax.rem(my_z, half) + delta_z, half)
+        y = lax.rem(my_y + rest // 2, blocks_y)
+        core = lax.rem(my_core + rest, 2)
         return (y * blocks_z + z) * 2 + core
 
+    def signal(semaphore, peer):
+        pl.semaphore_signal(semaphore, inc=1, device_id={"ctx": peer}, device_id_type=MESH)
+
+    def for_peers(base, action):
+        def one(step, carry):
+            action(peer_of(base, step))
+            return carry
+
+        lax.fori_loop(jnp.where(my_base == base, 1, 0), members, one, 0)
+
     barrier = pltpu.get_barrier_semaphore()
 
-    def greet(step, carry):
-        pl.semaphore_signal(
-            barrier, inc=1, device_id={"ctx": peer_of(step)}, device_id_type=MESH
-        )
-        return carry
-
-    lax.fori_loop(0, blocks - 1, greet, 0)
+    @pl.when(is_first)
+    def _():
+        for_peers(0, lambda peer: signal(barrier, peer))
+        for_peers(half, lambda peer: signal(barrier, peer))
 
     loads = []
     for place, (source, target) in enumerate(
@@ -139,6 +148,11 @@
         load = pltpu.make_async_copy(source, target, in_sems.at[place])
         load.start()
         loads.append(load)
+
+    @pl.when(jnp.logical_not(is_first))
+    def _():
+        pl.semaphore_wait(barrier, members)
+        for_peers(0, lambda peer: signal(ready_sem, peer))
 
     rate = rate_ref[...]
     residue = residue_ref[...]
@@ -165,11 +179,8 @@
             [gated, gate_grad], axis=1
         ).astype(BF16)
 
-    pl.semaphore_wait(barrier, blocks - 1)
-
-    def exchange(send, recv, phase):
-        def push(step, carry):
-            peer = peer_of(step)
+    def push(send, recv, phase, base):
+        def one(peer):
             pltpu.make_async_remote_copy(
                 src_ref=send.at[peer],
                 dst_ref=recv.at[me],
@@ -178,9 +189,10 @@
                 device_id={"ctx": peer},
                 device_id_type=MESH,
             ).start()
-            return carry
-
-        lax.fori_loop(0, blocks - 1, push, 0)
+
+        for_peers(base, one)
+
+    def keep(send, recv, phase):
         pltpu.make_async_copy(send.at[me], recv.at[me], recv_sems.at[phase]).start()
 
     def arrived(recv, phase):
@@ -190,7 +202,12 @@
         rest = send.at[pl.ds(0, blocks - 1)]
         pltpu.make_async_copy(rest, rest, send_sems.at[phase]).wait()
 
-    exchange(send_a, recv_a, 0)
+    @pl.when(is_first)
+    def _():
+        pl.semaphore_wait(barrier, members - 1)
+
+    push(send_a, recv_a, 0, 0)
+    keep(send_a, recv_a, 0)
 
     place_row = iota((BLOCK, LANES), 0).astype(F32)
     place_lane = iota((OWN, LANES), 1).astype(F32)
@@ -214,6 +231,29 @@
         toep_hi[channel] = high
         toep_lo[channel] = low
 
+    @pl.when(is_first)
+    def _():
+        pl.semaphore_wait(ready_sem, members)
+
+        def relay(z):
+            signal(relay_sem, (my_y * blocks_z + z) * 2 + my_core)
+
+        @pl.when(my_z == 0)
+        def _():
+            for z in range(half + half // 2, blocks_z):
+                relay(z)
+
+        @pl.when(my_z == half - 1)
+        def _():
+            for z in range(half, half + half // 2):
+                relay(z)
+
+    @pl.when(jnp.logical_not(is_first))
+    def _():
+        pl.semaphore_wait(relay_sem, 1)
+
+    push(send_a, recv_a, 0, half)
+
     arrived(recv_a, 0)
     wide[...] = recv_a[...].astype(F32).reshape(blocks * 16, BLOCK)
     for channel in range(OWN):
@@ -252,7 +292,9 @@
             dot(g_own, high, over) + dot(g_own, low, over) + g_carried[rows]
         )
     send_b[...] = wide[...].reshape(blocks, 16, BLOCK).astype(BF16)
-    exchange(send_b, recv_b, 1)
+    push(send_b, recv_b, 1, 0)
+    keep(send_b, recv_b, 1)
+    push(send_b, recv_b, 1, half)
 
     high, low = split(ahead * (float(BLOCK - 1) - place_row))
     x_slopes = own_rows(dot(x_all, high) + dot(x_all, low), blocks)
@@ -373,6 +415,8 @@
             pltpu.SemaphoreType.DMA((4,)),
             pltpu.SemaphoreType.DMA((2,)),
             pltpu.SemaphoreType.DMA((2,)),
+            pltpu.SemaphoreType.REGULAR,
+            pltpu.SemaphoreType.REGULAR,
         ],
         compiler_params=pltpu.CompilerParams(collective_id=0, has_side_effects=True, vmem_limit_bytes=60 * 1024 * 1024),
     )(query_proj, key_proj, value_proj, output_grad, residue, decay_rate)

time: 40.8 us -> 42.5 us (1.042); the launches traced: 40.1 us -> 42.4 us
  Pallas kernels: 39.4 us -> 41.7 us
    pallas_call x1, Pallas kernels: 38.6 us -> 40.9 us  [local(): pl.pallas_call(functools.partial(kernel, sizes, scale), out_shape=(tokens...]
where the time goes in v2:
time: 42.5 us; the launch traced here: 42.4 us
  Pallas kernels  41.7 us (98%)
  between operations  0.69 us (2%)
    pallas_call x1, Pallas kernels, local(): pl.pallas_call(functools.partial(kernel, sizes, scale), out_shape=(tokens...  40.9 us

profile of v2, /device:TPU:1, one launch (start us, length us, event | category | flops | bytes accessed | tf_op | source)
XLA Modules:
  0.0 42.4 jit_solution(3502570200174022130)
XLA Ops:
  0.6 0.0 copy-start
  0.6 0.0 copy-start.1
  0.7 0.0 copy-start.2
  0.7 40.9 %shard_map.101 = (bf16[128,512]{1,0:T(8,128)(2,1)S(1)}, bf16[128,512]{1,0:T(8,128)(2,1)S(1)}, f32[8,16]{1,0:T(8,128)S(1)}, f32[8,16]{1,0:T(8,128)S(1)}) custom-call(bf16[128,512]{1,0:T(8,128)(2,1)} %query_ref.1, bf16[128,512]{1,0:T(8,128)(2,1)} %key_ref.3, bf16[128,512]{1,0:T(8,128)(2,1)} %value_ref.3, bf16[128,512]{1,0:T(8,128)(2,1)} %upstream_ref.3, ...), custom_call_target="tpu_custom_call" | custom-call | tf_op jit(solution)/shard_map/pallas_call | solution.py:401
  41.5 0.0 copy-done
  41.5 0.0 copy-done.1
  41.6 0.0 copy-done.2
  41.6 0.8 %shard_map.102 = (bf16[128,512]{1,0:T(8,128)(2,1)}, bf16[128,512]{1,0:T(8,128)(2,1)}, bf16[128,512]{1,0:T(8,128)(2,1)}, f32[8,16]{1,0:T(8,128)}, f32[8,16]{1,0:T(8,128)}) custom-call(bf16[128,512]{1,0:T(8,128)(2,1)S(1)} %copy-done, bf16[128,512]{1,0:T(8,128)(2,1)S(1)} %copy-done.1, bf16[128,512]{1,0:T(8,128)(2,1)S(1)} %copy-done.2, ...), custom_call_target="tpu_custom_call" | custom-call | tf_op jit(solution)/shard_map/pallas_call | solution.py:423
Async XLA Ops:
  0.6 40.9 %copy-start = (bf16[128,512]{1,0:T(8,128)(2,1)S(1)}, bf16[128,512]{1,0:T(8,128)(2,1)}, u32[]{:S(2)}) copy-start(bf16[128,512]{1,0:T(8,128)(2,1)} %upstream_ref.3) | copy-start | bytes 393220
  0.6 40.9 %copy-start.1 = (bf16[128,512]{1,0:T(8,128)(2,1)S(1)}, bf16[128,512]{1,0:T(8,128)(2,1)}, u32[]{:S(2)}) copy-start(bf16[128,512]{1,0:T(8,128)(2,1)} %value_ref.3) | copy-start | bytes 393220
  0.7 40.9 %copy-start.2 = (bf16[128,512]{1,0:T(8,128)(2,1)S(1)}, bf16[128,512]{1,0:T(8,128)(2,1)}, u32[]{:S(2)}) copy-start(bf16[128,512]{1,0:T(8,128)(2,1)} %key_ref.3) | copy-start | bytes 393220

commit v3 on v1

--- a/solution.py
+++ b/solution.py
@@ -109,28 +109,39 @@
     my_z = lax.rem(me // 2, blocks_z)
     my_y = me // (2 * blocks_z)
 
-    def peer_of(step):
-        step_z = lax.rem(step, blocks_z)
-        rest = step // blocks_z
-        step_core = lax.rem(rest, 2)
-        step_y = rest // 2
-        half_z = (step_z + 1) // 2
-        delta_z = blocks_z // 2 + (1 - 2 * lax.rem(step_z, 2)) * half_z + blocks_z
-        delta_y = blocks_y - 1 - step_y
-        z = lax.rem(my_z + delta_z, blocks_z)
-        y = lax.rem(my_y + delta_y, blocks_y)
-        core = lax.rem(my_core + 1 + step_core, 2)
-        return (y * blocks_z + z) * 2 + core
+    half = blocks_z // 2
+
+    def for_plane(plane, action):
+        for step in range(2 * blocks_y):
+            y = lax.rem(my_y + step // 2, blocks_y)
+            core = lax.rem(my_core + step, 2)
+            peer = (y * blocks_z + plane) * 2 + core
+            if step == 0:
+                pl.when(plane != my_z)(functools.partial(action, peer))
+            else:
+                action(peer)
+
+    def for_far_first(action):
+        def one(step, carry):
+            delta = (1 - 2 * lax.rem(step, 2)) * ((step + 1) // 2)
+            for_plane(lax.rem(my_z + half + delta + blocks_z, blocks_z), action)
+            return carry
+
+        lax.fori_loop(0, blocks_z, one, 0)
+
+    def for_planes(first, last, action):
+        def one(plane, carry):
+            for_plane(plane, action)
+            return carry
+
+        lax.fori_loop(first, last, one, 0)
 
     barrier = pltpu.get_barrier_semaphore()
 
-    def greet(step, carry):
-        pl.semaphore_signal(
-            barrier, inc=1, device_id={"ctx": peer_of(step)}, device_id_type=MESH
-        )
-        return carry
-
-    lax.fori_loop(0, blocks - 1, greet, 0)
+    def greet(peer):
+        pl.semaphore_signal(barrier, inc=1, device_id={"ctx": peer}, device_id_type=MESH)
+
+    for_far_first(greet)
 
     loads = []
     for place, (source, target) in enumerate(
@@ -152,45 +163,47 @@
     rate_row = to_row(rate)
     gain_row = to_row(residue * jnp.sqrt(rate))
 
-    for load in loads:
-        load.wait()
     channels = blocks * OWN
-    for first in range(0, channels, LANES):
-        cols = pl.ds(first, LANES)
-        gated = (key_in[:, cols].astype(F32) * value_in[:, cols].astype(F32)).astype(BF16)
-        gate_grad = (upstream_in[:, cols].astype(F32) * query_in[:, cols].astype(F32)).astype(BF16)
-        gated = jnp.transpose(gated.astype(F32)).reshape(LANES // OWN, OWN, BLOCK)
-        gate_grad = jnp.transpose(gate_grad.astype(F32)).reshape(LANES // OWN, OWN, BLOCK)
-        send_a[pl.ds(first // OWN, LANES // OWN)] = jnp.concatenate(
-            [gated, gate_grad], axis=1
-        ).astype(BF16)
+    for array, (left, right) in enumerate(((key_in, value_in), (upstream_in, query_in))):
+        loads[2 * array].wait()
+        loads[2 * array + 1].wait()
+        for first in range(0, channels, LANES):
+            cols = pl.ds(first, LANES)
+            product = (left[:, cols].astype(F32) * right[:, cols].astype(F32)).astype(BF16)
+            send_a[array, pl.ds(first // OWN, LANES // OWN)] = (
+                jnp.transpose(product.astype(F32)).reshape(LANES // OWN, OWN, BLOCK).astype(BF16)
+            )
 
     pl.semaphore_wait(barrier, blocks - 1)
 
-    def exchange(send, recv, phase):
-        def push(step, carry):
-            peer = peer_of(step)
+    def pusher(send, recv, phase, array):
+        def push(peer):
             pltpu.make_async_remote_copy(
-                src_ref=send.at[peer],
-                dst_ref=recv.at[me],
-                send_sem=send_sems.at[phase],
-                recv_sem=recv_sems.at[phase],
+                src_ref=send.at[array, peer],
+                dst_ref=recv.at[array, me],
+                send_sem=send_sems.at[phase, array],
+                recv_sem=recv_sems.at[phase, array],
                 device_id={"ctx": peer},
                 device_id_type=MESH,
             ).start()
-            return carry
-
-        lax.fori_loop(0, blocks - 1, push, 0)
-        pltpu.make_async_copy(send.at[me], recv.at[me], recv_sems.at[phase]).start()
-
-    def arrived(recv, phase):
-        pltpu.make_async_copy(recv, recv, recv_sems.at[phase]).wait()
-
-    def sent(send, phase):
-        rest = send.at[pl.ds(0, blocks - 1)]
-        pltpu.make_async_copy(rest, rest, send_sems.at[phase]).wait()
-
-    exchange(send_a, recv_a, 0)
+
+        return push
+
+    def keep(send, recv, phase, array):
+        pltpu.make_async_copy(
+            send.at[array, me], recv.at[array, me], recv_sems.at[phase, array]
+        ).start()
+
+    def arrived(recv, phase, array):
+        pltpu.make_async_copy(recv.at[array], recv.at[array], recv_sems.at[phase, array]).wait()
+
+    def sent(send, phase, array):
+        rest = send.at[array, pl.ds(0, blocks - 1)]
+        pltpu.make_async_copy(rest, rest, send_sems.at[phase, array]).wait()
+
+    for array in range(2):
+        for_far_first(pusher(send_a, recv_a, 0, array))
+        keep(send_a, recv_a, 0, array)
 
     place_row = iota((BLOCK, LANES), 0).astype(F32)
     place_lane = iota((OWN, LANES), 1).astype(F32)
@@ -214,45 +227,47 @@
         toep_hi[channel] = high
         toep_lo[channel] = low
 
-    arrived(recv_a, 0)
-    wide[...] = recv_a[...].astype(F32).reshape(blocks * 16, BLOCK)
-    for channel in range(OWN):
-        rows = pl.ds(channel * blocks, blocks)
-        xs[rows, :] = wide[pl.ds(channel, blocks, stride=16), :].astype(BF16)
-        gs[rows, :] = wide[pl.ds(OWN + channel, blocks, stride=16), :].astype(BF16)
-    x_all = xs[...]
-    g_all = gs[...]
-    x_ends = own_rows(dot(x_all, tables[0]) + dot(x_all, tables[1]), blocks)
-    g_ends = own_rows(dot(g_all, tables[2]) + dot(g_all, tables[3]), blocks)
-    x_state = scan_blocks(x_ends, rate_row, True)
-    g_state = scan_blocks(g_ends, rate_row, False)
     group = iota((blocks, LANES), 1) // 16
 
-    def carried(state, high, low):
+    def own_signals(array, target):
+        arrived(recv_a, 0, array)
+        wide[...] = recv_a[array].astype(F32).reshape(blocks * OWN, BLOCK)
+        for channel in range(OWN):
+            target[pl.ds(channel * blocks, blocks), :] = wide[
+                pl.ds(channel, blocks, stride=OWN), :
+            ].astype(BF16)
+        return target[...]
+
+    def respond(array, signals, state, table, over):
+        high, low = tables[table], tables[table + 1]
         parts = jnp.concatenate(
             [jnp.where(group == channel, state, 0.0) for channel in range(OWN)], axis=0
         )
         part_hi, part_lo = split(parts)
-        over = ((1,), (1,))
-        return dot(part_hi, high, over) + dot(part_lo, high, over) + dot(part_hi, low, over)
-
-    x_carried = carried(x_state, tables[4], tables[5])
-    g_carried = carried(g_state, tables[6], tables[7])
-    for channel in range(OWN):
-        rows = slice(channel * blocks, (channel + 1) * blocks)
-        x_own = x_all[rows]
-        g_own = g_all[rows]
-        high = toep_hi[channel]
-        low = toep_lo[channel]
-        over = ((1,), (1,))
-        wide[pl.ds(channel, blocks, stride=16), :] = (
-            dot(x_own, high) + dot(x_own, low) + x_carried[rows]
-        )
-        wide[pl.ds(OWN + channel, blocks, stride=16), :] = (
-            dot(g_own, high, over) + dot(g_own, low, over) + g_carried[rows]
-        )
-    send_b[...] = wide[...].reshape(blocks, 16, BLOCK).astype(BF16)
-    exchange(send_b, recv_b, 1)
+        lanes = ((1,), (1,))
+        carried = dot(part_hi, high, lanes) + dot(part_lo, high, lanes) + dot(part_hi, low, lanes)
+        for channel in range(OWN):
+            rows = slice(channel * blocks, (channel + 1) * blocks)
+            wide[pl.ds(channel, blocks, stride=OWN), :] = (
+                dot(signals[rows], toep_hi[channel], over)
+                + dot(signals[rows], toep_lo[channel], over)
+                + carried[rows]
+            )
+        send_b[array] = wide[...].reshape(blocks, OWN, BLOCK).astype(BF16)
+
+    x_all = own_signals(0, xs)
+    x_ends = own_rows(dot(x_all, tables[0]) + dot(x_all, tables[1]), blocks)
+    x_state = scan_blocks(x_ends, rate_row, True)
+    respond(0, x_all, x_state, 4, ((1,), (0,)))
+    for_far_first(pusher(send_b, recv_b, 1, 0))
+    keep(send_b, recv_b, 1, 0)
+
+    g_all = own_signals(1, gs)
+    g_ends = own_rows(dot(g_all, tables[2]) + dot(g_all, tables[3]), blocks)
+    g_state = scan_blocks(g_ends, rate_row, False)
+    respond(1, g_all, g_state, 6, ((1,), (1,)))
+    for_far_first(pusher(send_b, recv_b, 1, 1))
+    keep(send_b, recv_b, 1, 1)
 
     high, low = split(ahead * (float(BLOCK - 1) - place_row))
     x_slopes = own_rows(dot(x_all, high) + dot(x_all, low), blocks)
@@ -291,14 +306,14 @@
     residue_grad_ref[...] = from_row(root_row * plain)
     rate_grad_ref[...] = from_row(root_row * residue_row * (0.5 * plain - rate_row * sloped))
 
-    arrived(recv_b, 1)
-    for first in range(0, channels, LANES):
-        cols = pl.ds(first, LANES)
-        both = recv_b[pl.ds(first // OWN, LANES // OWN)].astype(F32)
-        out_ref[:, cols] = jnp.transpose(both[:, :OWN].reshape(LANES, BLOCK)).astype(BF16)
-        grad_ref[:, cols] = jnp.transpose(both[:, OWN:].reshape(LANES, BLOCK)).astype(BF16)
-    sent(send_a, 0)
-    sent(send_b, 1)
+    for array, target in enumerate((out_ref, grad_ref)):
+        arrived(recv_b, 1, array)
+        for first in range(0, channels, LANES):
+            part = recv_b[array, pl.ds(first // OWN, LANES // OWN)].astype(F32)
+            target[:, pl.ds(first, LANES)] = jnp.transpose(part.reshape(LANES, BLOCK)).astype(BF16)
+    for array in range(2):
+        sent(send_a, 0, array)
+        sent(send_b, 1, array)
 
 
 def finish(
@@ -353,7 +368,7 @@
     vmem = pl.BlockSpec(memory_space=pltpu.VMEM)
     tokens = jax.ShapeDtypeStruct((tok_dev, channels), BF16)
     params = jax.ShapeDtypeStruct(residue.shape, F32)
-    message = pltpu.VMEM((blocks, 16, BLOCK), BF16)
+    message = pltpu.VMEM((2, blocks, OWN, BLOCK), BF16)
     tokens_vmem = pltpu.VMEM(tokens.shape, BF16)
     params_vmem = pltpu.VMEM(params.shape, F32)
     conv_out, conv_grad, residue_grad, rate_grad = pl.pallas_call(
@@ -364,15 +379,15 @@
         scratch_shapes=[pltpu.VMEM((tok_dev, channels), BF16)] * 4
         + [message] * 4
         + [
-            pltpu.VMEM((blocks * 16, BLOCK), F32),
+            pltpu.VMEM((blocks * OWN, BLOCK), F32),
             pltpu.VMEM((blocks * OWN, BLOCK), BF16),
             pltpu.VMEM((blocks * OWN, BLOCK), BF16),
             pltpu.VMEM((OWN, BLOCK, BLOCK), BF16),
             pltpu.VMEM((OWN, BLOCK, BLOCK), BF16),
             pltpu.VMEM((8, BLOCK, LANES), BF16),
             pltpu.SemaphoreType.DMA((4,)),
-            pltpu.SemaphoreType.DMA((2,)),
-            pltpu.SemaphoreType.DMA((2,)),
+            pltpu.SemaphoreType.DMA((2, 2)),
+            pltpu.SemaphoreType.DMA((2, 2)),
         ],
         compiler_params=pltpu.CompilerParams(collective_id=0, has_side_effects=True, vmem_limit_bytes=60 * 1024 * 1024),
     )(query_proj, key_proj, value_proj, output_grad, residue, decay_rate)

time: 40.8 us -> 38.7 us (0.949); the launches traced: 40.1 us -> 38.5 us
  Pallas kernels: 39.4 us -> 37.8 us
    pallas_call x1, Pallas kernels: 38.6 us -> 37 us  [local(): pl.pallas_call(functools.partial(kernel, sizes, scale), out_shape=(tokens...]
where the time goes in v3:
time: 38.7 us; the launch traced here: 38.5 us
  Pallas kernels  37.8 us (98%)
  between operations  0.69 us (2%)
    pallas_call x1, Pallas kernels, local(): pl.pallas_call(functools.partial(kernel, sizes, scale), out_shape=(tokens...  37 us
    pallas_call x1, Pallas kernels, local(): pl.pallas_call(finish, out_shape=(tokens,) * 3 + (params,) * 2, in_specs=...  0.82 us

profile of v3, /device:TPU:1, one launch (start us, length us, event | category | flops | bytes accessed | tf_op | source)
XLA Modules:
  0.0 38.5 jit_solution(5303989354422281126)
XLA Ops:
  0.6 0.0 copy-start
  0.6 0.0 copy-start.1
  0.7 0.0 copy-start.2
  0.7 37.0 %shard_map.101 = (bf16[128,512]{1,0:T(8,128)(2,1)S(1)}, bf16[128,512]{1,0:T(8,128)(2,1)S(1)}, f32[8,16]{1,0:T(8,128)S(1)}, f32[8,16]{1,0:T(8,128)S(1)}) custom-call(bf16[128,512]{1,0:T(8,128)(2,1)} %query_ref.1, bf16[128,512]{1,0:T(8,128)(2,1)} %key_ref.3, bf16[128,512]{1,0:T(8,128)(2,1)} %value_ref.3, bf16[128,512]{1,0:T(8,128)(2,1)} %upstream_ref.3, ...), custom_call_target="tpu_custom_call" | custom-call | tf_op jit(solution)/shard_map/pallas_call | solution.py:374
  37.7 0.0 copy-done
  37.7 0.0 copy-done.1
  37.7 0.0 copy-done.2
  37.7 0.8 %shard_map.102 = (bf16[128,512]{1,0:T(8,128)(2,1)}, bf16[128,512]{1,0:T(8,128)(2,1)}, bf16[128,512]{1,0:T(8,128)(2,1)}, f32[8,16]{1,0:T(8,128)}, f32[8,16]{1,0:T(8,128)}) custom-call(bf16[128,512]{1,0:T(8,128)(2,1)S(1)} %copy-done, bf16[128,512]{1,0:T(8,128)(2,1)S(1)} %copy-done.1, bf16[128,512]{1,0:T(8,128)(2,1)S(1)} %copy-done.2, ...), custom_call_target="tpu_custom_call" | custom-call | tf_op jit(solution)/shard_map/pallas_call | solution.py:394
Async XLA Ops:
  0.6 37.0 %copy-start = (bf16[128,512]{1,0:T(8,128)(2,1)S(1)}, bf16[128,512]{1,0:T(8,128)(2,1)}, u32[]{:S(2)}) copy-start(bf16[128,512]{1,0:T(8,128)(2,1)} %upstream_ref.3) | copy-start | bytes 393220
  0.6 37.0 %copy-start.1 = (bf16[128,512]{1,0:T(8,128)(2,1)S(1)}, bf16[128,512]{1,0:T(8,128)(2,1)}, u32[]{:S(2)}) copy-start(bf16[128,512]{1,0:T(8,128)(2,1)} %value_ref.3) | copy-start | bytes 393220
  0.7 37.0 %copy-start.2 = (bf16[128,512]{1,0:T(8,128)(2,1)S(1)}, bf16[128,512]{1,0:T(8,128)(2,1)}, u32[]{:S(2)}) copy-start(bf16[128,512]{1,0:T(8,128)(2,1)} %key_ref.3) | copy-start | bytes 393220

commit v4 on v3

--- a/solution.py
+++ b/solution.py
@@ -80,14 +80,17 @@
     upstream_ref,
     residue_ref,
     rate_ref,
-    out_ref,
-    grad_ref,
+    query_grad_ref,
+    key_grad_ref,
+    value_grad_ref,
     residue_grad_ref,
     rate_grad_ref,
     query_in,
     key_in,
     value_in,
     upstream_in,
+    residue_in,
+    rate_in,
     send_a,
     recv_a,
     send_b,
@@ -145,14 +148,23 @@
 
     loads = []
     for place, (source, target) in enumerate(
-        ((key_ref, key_in), (value_ref, value_in), (query_ref, query_in), (upstream_ref, upstream_in))
+        (
+            (key_ref, key_in),
+            (value_ref, value_in),
+            (query_ref, query_in),
+            (upstream_ref, upstream_in),
+            (residue_ref, residue_in),
+            (rate_ref, rate_in),
+        )
     ):
         load = pltpu.make_async_copy(source, target, in_sems.at[place])
         load.start()
         loads.append(load)
 
-    rate = rate_ref[...]
-    residue = residue_ref[...]
+    loads[4].wait()
+    loads[5].wait()
+    rate = rate_in[...]
+    residue = residue_in[...]
     spread = (iota((16, LANES), 1) % 16 == iota((16, LANES), 0)).astype(F32)
     own_lane = iota((OWN, LANES), 1) // 16 == iota((OWN, LANES), 0)
 
@@ -306,55 +318,31 @@
     residue_grad_ref[...] = from_row(root_row * plain)
     rate_grad_ref[...] = from_row(root_row * residue_row * (0.5 * plain - rate_row * sloped))
 
-    for array, target in enumerate((out_ref, grad_ref)):
+    products = (
+        ((upstream_in, query_grad_ref),),
+        ((value_in, key_grad_ref), (key_in, value_grad_ref)),
+    )
+    for array in range(2):
         arrived(recv_b, 1, array)
         for first in range(0, channels, LANES):
+            cols = pl.ds(first, LANES)
             part = recv_b[array, pl.ds(first // OWN, LANES // OWN)].astype(F32)
-            target[:, pl.ds(first, LANES)] = jnp.transpose(part.reshape(LANES, BLOCK)).astype(BF16)
+            part = jnp.transpose(part.reshape(LANES, BLOCK))
+            for gate, target in products[array]:
+                target[:, cols] = (gate[:, cols].astype(F32) * part).astype(BF16)
     for array in range(2):
         sent(send_a, 0, array)
         sent(send_b, 1, array)
 
 
-def finish(
-    upstream_ref,
-    value_ref,
-    key_ref,
-    out_ref,
-    grad_ref,
-    residue_grad_ref,
-    rate_grad_ref,
-    query_grad_hbm,
-    key_grad_hbm,
-    value_grad_hbm,
-    residue_grad_hbm,
-    rate_grad_hbm,
-    query_grad,
-    key_grad,
-    value_grad,
-    out_sems,
-):
+def finish(*refs):
+    count = len(refs) // 2
+    sources, targets, sems = refs[:count], refs[count:-1], refs[-1]
     stores = [
-        pltpu.make_async_copy(source, target, out_sems.at[place])
-        for place, (source, target) in enumerate(
-            (
-                (query_grad, query_grad_hbm),
-                (key_grad, key_grad_hbm),
-                (value_grad, value_grad_hbm),
-                (residue_grad_ref, residue_grad_hbm),
-                (rate_grad_ref, rate_grad_hbm),
-            )
-        )
+        pltpu.make_async_copy(source, target, sems.at[place])
+        for place, (source, target) in enumerate(zip(sources, targets))
     ]
-    stores[3].start()
-    stores[4].start()
-    products = (
-        (upstream_ref, out_ref, query_grad),
-        (value_ref, grad_ref, key_grad),
-        (key_ref, grad_ref, value_grad),
-    )
-    for store, (gate, result, target) in zip(stores, products):
-        target[...] = (gate[...].astype(F32) * result[...].astype(F32)).astype(BF16)
+    for store in stores:
         store.start()
     for store in stores:
         store.wait()
@@ -371,12 +359,13 @@
     message = pltpu.VMEM((2, blocks, OWN, BLOCK), BF16)
     tokens_vmem = pltpu.VMEM(tokens.shape, BF16)
     params_vmem = pltpu.VMEM(params.shape, F32)
-    conv_out, conv_grad, residue_grad, rate_grad = pl.pallas_call(
+    results = pl.pallas_call(
         functools.partial(kernel, sizes, scale),
-        out_shape=(tokens_vmem, tokens_vmem, params_vmem, params_vmem),
-        in_specs=[anywhere] * 4 + [vmem] * 2,
-        out_specs=[vmem] * 4,
+        out_shape=(tokens_vmem,) * 3 + (params_vmem,) * 2,
+        in_specs=[anywhere] * 6,
+        out_specs=[vmem] * 5,
         scratch_shapes=[pltpu.VMEM((tok_dev, channels), BF16)] * 4
+        + [params_vmem] * 2
         + [message] * 4
         + [
             pltpu.VMEM((blocks * OWN, BLOCK), F32),
@@ -385,7 +374,7 @@
             pltpu.VMEM((OWN, BLOCK, BLOCK), BF16),
             pltpu.VMEM((OWN, BLOCK, BLOCK), BF16),
             pltpu.VMEM((8, BLOCK, LANES), BF16),
-            pltpu.SemaphoreType.DMA((4,)),
+            pltpu.SemaphoreType.DMA((6,)),
             pltpu.SemaphoreType.DMA((2, 2)),
             pltpu.SemaphoreType.DMA((2, 2)),
         ],
@@ -394,12 +383,11 @@
     return pl.pallas_call(
         finish,
         out_shape=(tokens,) * 3 + (params,) * 2,
-        in_specs=[vmem] * 7,
+        in_specs=[vmem] * 5,
         out_specs=[anywhere] * 5,
-        scratch_shapes=[pltpu.VMEM((tok_dev, channels), BF16)] * 3
-        + [pltpu.SemaphoreType.DMA((5,))],
+        scratch_shapes=[pltpu.SemaphoreType.DMA((5,))],
         compiler_params=pltpu.CompilerParams(vmem_limit_bytes=8 << 20),
-    )(output_grad, value_proj, key_proj, conv_out, conv_grad, residue_grad, rate_grad)
+    )(*results)
 
 
 def solution(mesh):

time: 38.7 us -> 37.7 us (0.974)
  Pallas kernels: 37.8 us -> 36.9 us
    pallas_call x1, Pallas kernels: 37 us -> 36.1 us  [local(): pl.pallas_call(functools.partial(kernel, sizes, scale), out_shape=(tokens...]
where the time goes in v4:
time: 37.7 us; the launch traced here: 37.5 us
  Pallas kernels  36.9 us (98%)
  between operations  0.64 us (2%)
    pallas_call x1, Pallas kernels, local(): pl.pallas_call(functools.partial(kernel, sizes, scale), out_shape=(tokens...  36.1 us
    pallas_call x1, Pallas kernels, local(): pl.pallas_call(finish, out_shape=(tokens,) * 3 + (params,) * 2, in_specs=...  0.79 us

profile of v4, /device:TPU:1, one launch (start us, length us, event | category | flops | bytes accessed | tf_op | source)
XLA Modules:
  0.0 37.5 jit_solution(2188425658281068808)
XLA Ops:
  0.6 36.1 %shard_map.101 = (bf16[128,512]{1,0:T(8,128)(2,1)S(1)}, bf16[128,512]{1,0:T(8,128)(2,1)S(1)}, bf16[128,512]{1,0:T(8,128)(2,1)S(1)}, f32[8,16]{1,0:T(8,128)S(1)}, f32[8,16]{1,0:T(8,128)S(1)}) custom-call(bf16[128,512]{1,0:T(8,128)(2,1)} %query_ref.1, bf16[128,512]{1,0:T(8,128)(2,1)} %key_ref.1, bf16[128,512]{1,0:T(8,128)(2,1)} %value_ref.1, ...), custom_call_target="tpu_custom_call" | custom-call | tf_op jit(solution)/shard_map/pallas_call | solution.py:362
  36.7 0.8 %shard_map.102 = (bf16[128,512]{1,0:T(8,128)(2,1)}, bf16[128,512]{1,0:T(8,128)(2,1)}, bf16[128,512]{1,0:T(8,128)(2,1)}, f32[8,16]{1,0:T(8,128)}, f32[8,16]{1,0:T(8,128)}) custom-call(bf16[128,512]{1,0:T(8,128)(2,1)S(1)} %get-tuple-element.10.refs_0_, bf16[128,512]{1,0:T(8,128)(2,1)S(1)} %get-tuple-element.11.refs_1_, ...), custom_call_target="tpu_custom_call" | custom-call | tf_op jit(solution)/shard_map/pallas_call | solution.py:383

commit v5 on v4

--- a/solution.py
+++ b/solution.py
@@ -98,8 +98,9 @@
     wide,
     xs,
     gs,
-    toep_hi,
-    toep_lo,
+    toep_x,
+    toep_g,
+    end_tables,
     tables,
     in_sems,
     send_sems,
@@ -114,30 +115,19 @@
 
     half = blocks_z // 2
 
-    def for_plane(plane, action):
-        for step in range(2 * blocks_y):
-            y = lax.rem(my_y + step // 2, blocks_y)
-            core = lax.rem(my_core + step, 2)
-            peer = (y * blocks_z + plane) * 2 + core
-            if step == 0:
-                pl.when(plane != my_z)(functools.partial(action, peer))
-            else:
-                action(peer)
-
     def for_far_first(action):
-        def one(step, carry):
-            delta = (1 - 2 * lax.rem(step, 2)) * ((step + 1) // 2)
-            for_plane(lax.rem(my_z + half + delta + blocks_z, blocks_z), action)
-            return carry
-
-        lax.fori_loop(0, blocks_z, one, 0)
-
-    def for_planes(first, last, action):
-        def one(plane, carry):
-            for_plane(plane, action)
-            return carry
-
-        lax.fori_loop(first, last, one, 0)
+        def hops(offset):
+            y, z, _ = offset
+            return 2 * min(y, blocks_y - y) + min(z, blocks_z - z)
+
+        ways = [0]
+        for z in range(1, half):
+            ways += [z, blocks_z - z]
+        ways.append(half)
+        offsets = [(y, z, core) for z in ways for core in range(2) for y in range(blocks_y)]
+        for y, z, core in sorted(offsets[1:], key=hops, reverse=True):
+            chip = lax.rem(my_y + y, blocks_y) * blocks_z + lax.rem(my_z + z, blocks_z)
+            action(chip * 2 + lax.rem(my_core + core, 2))
 
     barrier = pltpu.get_barrier_semaphore()
 
@@ -216,15 +206,18 @@
     for array in range(2):
         for_far_first(pusher(send_a, recv_a, 0, array))
         keep(send_a, recv_a, 0, array)
+        if array == 0:
+            sent(send_a, 0, 0)
 
     place_row = iota((BLOCK, LANES), 0).astype(F32)
     place_lane = iota((OWN, LANES), 1).astype(F32)
     ahead = jnp.exp(-rate_row * (float(BLOCK - 1) - place_row))
     behind = jnp.exp(-rate_row * (place_row + 1.0))
-    for place, table in enumerate((ahead, behind, gain_row * behind, gain_row * ahead)):
+    for place, table in enumerate((ahead, behind)):
+        end_tables[place] = jnp.concatenate(split(table), axis=0)
+    for place, table in enumerate((gain_row * behind, gain_row * ahead)):
         high, low = split(table)
-        tables[2 * place] = high
-        tables[2 * place + 1] = low
+        tables[place] = jnp.concatenate([high, high, low], axis=1)
     taps = jnp.zeros((OWN, LANES), F32)
     for mode in range(16):
         mode_rate = rate[:, mode : mode + 1]
@@ -236,8 +229,8 @@
         row = jnp.broadcast_to(taps[channel : channel + 1], (BLOCK, LANES))
         row = pltpu.roll(row, 0, 1, stride=1, stride_axis=0)
         high, low = split(jnp.where(causal, row, 0.0))
-        toep_hi[channel] = high
-        toep_lo[channel] = low
+        toep_x[channel] = jnp.concatenate([high, low], axis=0)
+        toep_g[channel] = jnp.concatenate([high, low], axis=1)
 
     group = iota((blocks, LANES), 1) // 16
 
@@ -250,34 +243,33 @@
             ].astype(BF16)
         return target[...]
 
-    def respond(array, signals, state, table, over):
-        high, low = tables[table], tables[table + 1]
+    def twice(signals):
+        return jnp.concatenate([signals, signals], axis=1)
+
+    def respond(array, signals, state, toep, over):
         parts = jnp.concatenate(
             [jnp.where(group == channel, state, 0.0) for channel in range(OWN)], axis=0
         )
-        part_hi, part_lo = split(parts)
-        lanes = ((1,), (1,))
-        carried = dot(part_hi, high, lanes) + dot(part_lo, high, lanes) + dot(part_hi, low, lanes)
+        high, low = split(parts)
+        carried = dot(jnp.concatenate([high, low, high], axis=1), tables[array], ((1,), (1,)))
         for channel in range(OWN):
             rows = slice(channel * blocks, (channel + 1) * blocks)
             wide[pl.ds(channel, blocks, stride=OWN), :] = (
-                dot(signals[rows], toep_hi[channel], over)
-                + dot(signals[rows], toep_lo[channel], over)
-                + carried[rows]
+                dot(twice(signals[rows]), toep[channel], over) + carried[rows]
             )
         send_b[array] = wide[...].reshape(blocks, OWN, BLOCK).astype(BF16)
 
     x_all = own_signals(0, xs)
-    x_ends = own_rows(dot(x_all, tables[0]) + dot(x_all, tables[1]), blocks)
+    x_ends = own_rows(dot(twice(x_all), end_tables[0]), blocks)
     x_state = scan_blocks(x_ends, rate_row, True)
-    respond(0, x_all, x_state, 4, ((1,), (0,)))
+    respond(0, x_all, x_state, toep_x, ((1,), (0,)))
     for_far_first(pusher(send_b, recv_b, 1, 0))
     keep(send_b, recv_b, 1, 0)
 
     g_all = own_signals(1, gs)
-    g_ends = own_rows(dot(g_all, tables[2]) + dot(g_all, tables[3]), blocks)
+    g_ends = own_rows(dot(twice(g_all), end_tables[1]), blocks)
     g_state = scan_blocks(g_ends, rate_row, False)
-    respond(1, g_all, g_state, 6, ((1,), (1,)))
+    respond(1, g_all, g_state, toep_g, ((1,), (1,)))
     for_far_first(pusher(send_b, recv_b, 1, 1))
     keep(send_b, recv_b, 1, 1)
 
@@ -330,8 +322,8 @@
             part = jnp.transpose(part.reshape(LANES, BLOCK))
             for gate, target in products[array]:
                 target[:, cols] = (gate[:, cols].astype(F32) * part).astype(BF16)
+    sent(send_a, 0, 1)
     for array in range(2):
-        sent(send_a, 0, array)
         sent(send_b, 1, array)
 
 
@@ -371,9 +363,10 @@
             pltpu.VMEM((blocks * OWN, BLOCK), F32),
             pltpu.VMEM((blocks * OWN, BLOCK), BF16),
             pltpu.VMEM((blocks * OWN, BLOCK), BF16),
-            pltpu.VMEM((OWN, BLOCK, BLOCK), BF16),
-            pltpu.VMEM((OWN, BLOCK, BLOCK), BF16),
-            pltpu.VMEM((8, BLOCK, LANES), BF16),
+            pltpu.VMEM((OWN, 2 * BLOCK, BLOCK), BF16),
+            pltpu.VMEM((OWN, BLOCK, 2 * BLOCK), BF16),
+            pltpu.VMEM((2, 2 * BLOCK, LANES), BF16),
+            pltpu.VMEM((2, BLOCK, 3 * LANES), BF16),
             pltpu.SemaphoreType.DMA((6,)),
             pltpu.SemaphoreType.DMA((2, 2)),
             pltpu.SemaphoreType.DMA((2, 2)),

time: 37.7 us -> 36.9 us (0.979)
  Pallas kernels: 36.9 us -> 36.1 us
    pallas_call x1, Pallas kernels: 36.1 us -> 35.3 us  [local(): pl.pallas_call(functools.partial(kernel, sizes, scale), out_shape=(tokens...]
where the time goes in v5:
time: 36.9 us; the launch traced here: 36.7 us
  Pallas kernels  36.1 us (98%)
  between operations  0.64 us (2%)
    pallas_call x1, Pallas kernels, local(): pl.pallas_call(functools.partial(kernel, sizes, scale), out_shape=(tokens...  35.3 us
    pallas_call x1, Pallas kernels, local(): pl.pallas_call(finish, out_shape=(tokens,) * 3 + (params,) * 2, in_specs=...  0.79 us

profile of v5, /device:TPU:1, one launch (start us, length us, event | category | flops | bytes accessed | tf_op | source)
XLA Modules:
  0.0 36.7 jit_solution(3652034351071799158)
XLA Ops:
  0.6 35.3 %shard_map.101 = (bf16[128,512]{1,0:T(8,128)(2,1)S(1)}, bf16[128,512]{1,0:T(8,128)(2,1)S(1)}, bf16[128,512]{1,0:T(8,128)(2,1)S(1)}, f32[8,16]{1,0:T(8,128)S(1)}, f32[8,16]{1,0:T(8,128)S(1)}) custom-call(bf16[128,512]{1,0:T(8,128)(2,1)} %query_ref.1, bf16[128,512]{1,0:T(8,128)(2,1)} %key_ref.1, bf16[128,512]{1,0:T(8,128)(2,1)} %value_ref.1, ...), custom_call_target="tpu_custom_call" | custom-call | tf_op jit(solution)/shard_map/pallas_call | solution.py:354
  35.9 0.8 %shard_map.102 = (bf16[128,512]{1,0:T(8,128)(2,1)}, bf16[128,512]{1,0:T(8,128)(2,1)}, bf16[128,512]{1,0:T(8,128)(2,1)}, f32[8,16]{1,0:T(8,128)}, f32[8,16]{1,0:T(8,128)}) custom-call(bf16[128,512]{1,0:T(8,128)(2,1)S(1)} %get-tuple-element.10.refs_0_, bf16[128,512]{1,0:T(8,128)(2,1)S(1)} %get-tuple-element.11.refs_1_, ...), custom_call_target="tpu_custom_call" | custom-call | tf_op jit(solution)/shard_map/pallas_call | solution.py:376

commit v6 on v5

--- a/solution.py
+++ b/solution.py
@@ -96,8 +96,6 @@
     send_b,
     recv_b,
     wide,
-    xs,
-    gs,
     toep_x,
     toep_g,
     end_tables,
@@ -234,14 +232,13 @@
 
     group = iota((blocks, LANES), 1) // 16
 
-    def own_signals(array, target):
+    def own_signals(array):
         arrived(recv_a, 0, array)
         wide[...] = recv_a[array].astype(F32).reshape(blocks * OWN, BLOCK)
-        for channel in range(OWN):
-            target[pl.ds(channel * blocks, blocks), :] = wide[
-                pl.ds(channel, blocks, stride=OWN), :
-            ].astype(BF16)
-        return target[...]
+        return jnp.concatenate(
+            [wide[pl.ds(channel, blocks, stride=OWN), :].astype(BF16) for channel in range(OWN)],
+            axis=0,
+        )
 
     def twice(signals):
         return jnp.concatenate([signals, signals], axis=1)
@@ -259,14 +256,14 @@
             )
         send_b[array] = wide[...].reshape(blocks, OWN, BLOCK).astype(BF16)
 
-    x_all = own_signals(0, xs)
+    x_all = own_signals(0)
     x_ends = own_rows(dot(twice(x_all), end_tables[0]), blocks)
     x_state = scan_blocks(x_ends, rate_row, True)
     respond(0, x_all, x_state, toep_x, ((1,), (0,)))
     for_far_first(pusher(send_b, recv_b, 1, 0))
     keep(send_b, recv_b, 1, 0)
 
-    g_all = own_signals(1, gs)
+    g_all = own_signals(1)
     g_ends = own_rows(dot(twice(g_all), end_tables[1]), blocks)
     g_state = scan_blocks(g_ends, rate_row, False)
     respond(1, g_all, g_state, toep_g, ((1,), (1,)))
@@ -361,8 +358,6 @@
         + [message] * 4
         + [
             pltpu.VMEM((blocks * OWN, BLOCK), F32),
-            pltpu.VMEM((blocks * OWN, BLOCK), BF16),
-            pltpu.VMEM((blocks * OWN, BLOCK), BF16),
             pltpu.VMEM((OWN, 2 * BLOCK, BLOCK), BF16),
             pltpu.VMEM((OWN, BLOCK, 2 * BLOCK), BF16),
             pltpu.VMEM((2, 2 * BLOCK, LANES), BF16),

time: 36.9 us -> 36.9 us (level)
  no operation moved by 1% of the time
where the time goes in v6:
time: 36.9 us; the launch traced here: 36.7 us
  Pallas kernels  36.1 us (98%)
  between operations  0.64 us (2%)
    pallas_call x1, Pallas kernels, local(): pl.pallas_call(functools.partial(kernel, sizes, scale), out_shape=(tokens...  35.3 us
    pallas_call x1, Pallas kernels, local(): pl.pallas_call(finish, out_shape=(tokens,) * 3 + (params,) * 2, in_specs=...  0.79 us

profile of v6, /device:TPU:1, one launch (start us, length us, event | category | flops | bytes accessed | tf_op | source)
XLA Modules:
  0.0 36.7 jit_solution(3219050275441974015)
XLA Ops:
  0.6 35.3 %shard_map.101 = (bf16[128,512]{1,0:T(8,128)(2,1)S(1)}, bf16[128,512]{1,0:T(8,128)(2,1)S(1)}, bf16[128,512]{1,0:T(8,128)(2,1)S(1)}, f32[8,16]{1,0:T(8,128)S(1)}, f32[8,16]{1,0:T(8,128)S(1)}) custom-call(bf16[128,512]{1,0:T(8,128)(2,1)} %query_ref.1, bf16[128,512]{1,0:T(8,128)(2,1)} %key_ref.1, bf16[128,512]{1,0:T(8,128)(2,1)} %value_ref.1, ...), custom_call_target="tpu_custom_call" | custom-call | tf_op jit(solution)/shard_map/pallas_call | solution.py:351
  35.9 0.8 %shard_map.102 = (bf16[128,512]{1,0:T(8,128)(2,1)}, bf16[128,512]{1,0:T(8,128)(2,1)}, bf16[128,512]{1,0:T(8,128)(2,1)}, f32[8,16]{1,0:T(8,128)}, f32[8,16]{1,0:T(8,128)}) custom-call(bf16[128,512]{1,0:T(8,128)(2,1)S(1)} %get-tuple-element.10.refs_0_, bf16[128,512]{1,0:T(8,128)(2,1)S(1)} %get-tuple-element.11.refs_1_, ...), custom_call_target="tpu_custom_call" | custom-call | tf_op jit(solution)/shard_map/pallas_call | solution.py:371
